TPU v7x, 256 devices: a whole 4x4x8 slice. The times are simulated.
256 devices in a mesh: seq: 32 (over y, x, core), grp: 8 (over z).
Axes of the slice: x: 4, y: 4, z: 8, core: 2. Of those that a mesh axis runs over, the one named last changes fastest.
Arguments:
- hidden_in: bfloat16 [98304, 2048], P(('grp', 'seq')), parts along dimension 0, may hold values from -8 to 8
- norm_gain: bfloat16 [2048], replicated, may hold values from 0.099609375 to 1.8984375
- w_query: bfloat16 [2048, 2048], P('seq'), may hold values from -1 to 1
- w_key: bfloat16 [2048, 128], P('seq'), may hold values from -1 to 1
- w_value: bfloat16 [2048, 128], P('seq'), may hold values from -0.125 to 0.125
- w_out: bfloat16 [2048, 2048], P('seq'), may hold values from -0.625 to 0.625
- seg_ids: int32 [98304], P('grp'), parts along dimension 0, may hold values from 0 to 1, never falling along the last dimension, each value on 1 to 11904 neighbouring positions
- cache_slot: int32 [768], P('grp'), parts along dimension 0, may hold values from 0 to 95, each once
Outputs:
- hidden_out: bfloat16 [98304, 2048], P(('grp', 'seq')), parts along dimension 0
- kv_cache: bfloat16 [98304, 256], P(('grp', 'seq')), parts along dimension 0
There are 8 independent parts, one for each index of `grp`. A program takes and returns all parts, laid end to end along the dimension named above; an argument that names none is the same for every part. Nothing has to cross between parts.
Inputs may be any that keep to these rules, and one draw needn't show every extreme that they name: `seg_ids`: segment numbers never fall along the stream; each prompt holds 1 to 11904 tokens. `cache_slot`: every cache position appears exactly once.
All inputs are finite; a program needn't handle non-finite values.
Results may differ from a plain program's by a relative error of at most 0.01.
Values may be sent and summed in bfloat16 or wider, within the bound.
No kernel may reach another device: no remote copies, remote signals or barrier semaphores. Data moves between devices by JAX's collectives and lax.ppermute only.
A program may use at most 256 MiB of HBM per device.

v0:
```python
import jax
import jax.numpy as jnp
from jax import lax
from jax.sharding import PartitionSpec as P

WINDOW = 1024
CACHE_BLK = 128
REACH = 3
EPSILON = 1e-06


def shifted(array, axis, by):
    length = lax.axis_size(axis)
    pairs = [(i, i + by) for i in range(length) if 0 <= i + by < length]
    return lax.ppermute(array, axis, pairs)


def normalize(hidden_in, norm_gain):
    values_wide = hidden_in.astype(jnp.float32)
    mean_square = jnp.mean(values_wide * values_wide, axis=1, keepdims=True)
    return (values_wide * lax.rsqrt(mean_square + EPSILON) * norm_gain.astype(jnp.float32)).astype(
        jnp.bfloat16
    )


def attend_block(queries, key_rows, value_rows, seg_query, seg_key, pos_query, pos_key):
    row_count = queries.shape[0]
    head_dim = key_rows.shape[1]
    head_count = queries.shape[1] // head_dim
    visible = (
        (seg_query[:, None] == seg_key[None, :])
        & (pos_key[None, :] <= pos_query[:, None])
        & (pos_key[None, :] > pos_query[:, None] - WINDOW)
    )
    score_scale = 1.0 / head_dim**0.5

    def one_head(query_head):
        scores = (
            lax.dot_general(
                query_head, key_rows, (((1,), (1,)), ((), ())), preferred_element_type=jnp.float32
            )
            * score_scale
        )
        scores = jnp.where(visible, scores, -jnp.inf)
        row_top = jnp.max(scores, axis=1, keepdims=True)
        weights = jnp.exp(scores - row_top).astype(jnp.bfloat16)
        weight_sum = jnp.sum(weights.astype(jnp.float32), axis=1, keepdims=True)
        mixture = jnp.dot(weights, value_rows, preferred_element_type=jnp.float32) / weight_sum
        return mixture.astype(jnp.bfloat16)

    per_head = jnp.transpose(queries.reshape(row_count, head_count, head_dim), (1, 0, 2))
    result = lax.map(one_head, per_head)
    return jnp.transpose(result, (1, 0, 2)).reshape(row_count, head_count * head_dim)


def shards(hidden_in, norm_gain, w_query, w_key, w_value, w_out, seg_ids, cache_slot):
    row_count = hidden_in.shape[0]
    devices = lax.axis_size("seq")
    my_index = lax.axis_index("seq")
    normed = normalize(hidden_in, norm_gain)
    head_dim = w_key.shape[1]
    pieces = (
        lax.all_gather(w_query, "seq", axis=0, tiled=True),
        lax.all_gather(w_key, "seq", axis=0, tiled=True),
        lax.all_gather(w_value, "seq", axis=0, tiled=True),
    )
    columns = normed
    query_sum, key_sum, value_sum = tuple(
        (jnp.dot(columns, piece, preferred_element_type=jnp.float32) for piece in pieces)
    )
    query = query_sum.astype(jnp.bfloat16)
    stacked = jnp.concatenate(
        [key_sum.astype(jnp.bfloat16), value_sum.astype(jnp.bfloat16)], axis=1
    )
    margin = REACH * row_count
    span = (REACH + 1) * row_count
    reach_now = min(REACH, devices - 1)
    missing = jnp.zeros(((REACH - reach_now) * row_count, 2 * head_dim), jnp.bfloat16)
    received = []
    current = stacked
    for distance in range(reach_now):
        current = shifted(current, "seq", 1)
        received.append(current)
    window_rows = jnp.concatenate([missing] + received[::-1] + [stacked], axis=0)
    first_row = my_index * row_count
    seg_pad = jnp.concatenate([jnp.full((margin,), -1, jnp.int32), seg_ids])
    seg_query = lax.dynamic_slice_in_dim(seg_ids, first_row, row_count, 0)
    seg_key = lax.dynamic_slice_in_dim(seg_pad, first_row, span, 0)
    pos_query = first_row + jnp.arange(row_count, dtype=jnp.int32)
    pos_key = first_row - margin + jnp.arange(span, dtype=jnp.int32)
    attended = attend_block(
        query,
        window_rows[:, :head_dim],
        window_rows[:, head_dim:],
        seg_query,
        seg_key,
        pos_query,
        pos_key,
    )
    columns = attended
    projected = jnp.dot(
        columns,
        lax.all_gather(w_out, "seq", axis=0, tiled=True),
        preferred_element_type=jnp.float32,
    )
    hidden_out = (hidden_in.astype(jnp.float32) + projected).astype(jnp.bfloat16)
    blocks_per_dev = row_count // CACHE_BLK
    block_total = cache_slot.shape[0]
    slot_ids = jnp.arange(block_total, dtype=jnp.int32)
    source_of = jnp.sum(
        jnp.where(cache_slot[None, :] == slot_ids[:, None], slot_ids[None, :], 0), axis=1
    )
    owned_sources = lax.dynamic_slice_in_dim(
        source_of, my_index * blocks_per_dev, blocks_per_dev, 0
    )
    within = jnp.arange(row_count, dtype=jnp.int32)
    source_row = (
        jnp.repeat(owned_sources, CACHE_BLK, total_repeat_length=row_count) * CACHE_BLK
        + within % CACHE_BLK
    )
    piece = lax.all_gather(stacked, "seq", axis=0, tiled=True)
    inside = (source_row >= 0) & (source_row < piece.shape[0])
    taken = jnp.take(piece, jnp.clip(source_row, 0, piece.shape[0] - 1), axis=0)
    kv_cache = jnp.where(inside[:, None], taken, jnp.zeros_like(stacked))
    return (hidden_out, kv_cache)


def solution(mesh):
    in_specs = (
        P(("grp", "seq"), None),
        P(),
        P("seq", None),
        P("seq", None),
        P("seq", None),
        P("seq", None),
        P("grp"),
        P("grp"),
    )
    out_specs = (P(("grp", "seq"), None), P(("grp", "seq"), None))
    return jax.shard_map(shards, mesh=mesh, in_specs=in_specs, out_specs=out_specs, check_vma=False)
```

profile of v0, /device:TPU:1, one launch (start us, length us, event | category | flops | bytes accessed | tf_op | source)
XLA Modules:
  0.0 271.4 jit_solution(2322478954140555485)
XLA Ops:
  7.2 0.8 convert_element_type.32
  8.0 1.8 fusion.8
  9.8 26.4 %all_gather.17 = bf16[2048,128]{1,0:T(8,128)(2,1)S(1)} all-gather(bf16[64,128]{1,0:T(8,128)(2,1)} %param.16), channel_id=1, replica_groups=mesh['seq'=32,'grp'=8] {'seq'}, dimensions={0}, use_global_device_ids=true | all-gather | bytes 540672 | tf_op jit(solution)/shard_map/all_gather | solution.py:65
  36.3 24.1 %all_gather.16 = bf16[2048,128]{1,0:T(8,128)(2,1)S(1)} all-gather(bf16[64,128]{1,0:T(8,128)(2,1)} %param.15), channel_id=1, replica_groups=mesh['seq'=32,'grp'=8] {'seq'}, dimensions={0}, use_global_device_ids=true | all-gather | bytes 540672 | tf_op jit(solution)/shard_map/all_gather | solution.py:64
  60.4 0.7 convolution_convert_fusion.1
  61.1 0.7 convolution_convert_fusion.2
  61.9 0.7 pad_maximum_fusion
  62.6 0.7 all-gather.4.cloned.1.call-update
  63.4 1.9 collective-permute-start
  65.6 0.7 fusion.30
  66.3 2.0 fusion.23
  68.4 4.1 %collective-permute-start.1 = (bf16[384,256]{0,1:T(8,128)(2,1)S(1)}, bf16[384,256]{0,1:T(8,128)(2,1)S(1)}, u32[]{:S(2)}, u32[]{:S(2)}) collective-permute-start(bf16[384,256]{0,1:T(8,128)(2,1)S(1)} %collective-permute-done), channel_id=1, source_target_pairs={{0,8},{8,16},{16,24},{24,32},{32,40},{40,48},{48,56},{56,64},{64,7... | collective-permute-start | bytes 589832 | tf_op jit(solution)/shard_map/ppermute | solution.py:15
  72.5 2.6 collective-permute-done.1
  75.1 4.6 %collective-permute-start.2 = (bf16[384,256]{0,1:T(8,128)(2,1)S(1)}, bf16[384,256]{0,1:T(8,128)(2,1)S(1)}, u32[]{:S(2)}, u32[]{:S(2)}) collective-permute-start(bf16[384,256]{0,1:T(8,128)(2,1)S(1)} %collective-permute-done.1), channel_id=1, source_target_pairs={{0,8},{8,16},{16,24},{24,32},{32,40},{40,48},{48,56},{56,64},{64,7... | collective-permute-start | bytes 589832 | tf_op jit(solution)/shard_map/ppermute | solution.py:15
  79.7 3.3 %collective-permute-done.2 = bf16[384,256]{0,1:T(8,128)(2,1)S(1)} collective-permute-done((bf16[384,256]{0,1:T(8,128)(2,1)S(1)}, bf16[384,256]{0,1:T(8,128)(2,1)S(1)}, u32[]{:S(2)}, u32[]{:S(2)}) %collective-permute-start.2) | collective-permute-done | bytes 196640 | tf_op jit(solution)/shard_map/ppermute | solution.py:15
  83.1 0.9 copy.20
  84.0 0.9 copy.21
  84.9 37.7 %all-gather.8.cloned.1.call-done = bf16[12288,256]{0,1:T(8,128)(2,1)} async-done(((bf16[384,256]{0,1:T(8,128)(2,1)}), bf16[12288,256]{0,1:T(8,128)(2,1)}) %all-gather.8.cloned.1.call-update) | async-done | bytes 6291472 | tf_op jit(solution)/shard_map/all_gather | solution.py:121
  122.7 8.6 %copy.23 = bf16[12288,256]{1,0:T(8,128)(2,1)} copy(bf16[12288,256]{0,1:T(8,128)(2,1)} %all-gather.8.cloned.1.call-done) | data formatting | bytes 12582912 | tf_op jit(solution)/shard_map/all_gather | solution.py:121
  131.3 5.3 %gather_fusion = bf16[384,256]{1,0:T(8,128)(2,1)S(1)} fusion(bf16[12288,256]{1,0:T(8,128)(2,1)} %copy.23, s32[1024]{0:T(1024)S(1)} %pad_clamp_fusion), kind=kCustom, calls=%fused_computation | custom fusion | bytes 394752 | tf_op jit(solution)/shard_map/jit(_take)/gather | solution.py:123
  136.6 0.8 select_select_fusion
  137.4 45.4 %all-gather.4.cloned.1.call-done = bf16[2048,2048]{1,0:T(8,128)(2,1)} async-done(((bf16[64,2048]{1,0:T(8,128)(2,1)}), bf16[2048,2048]{1,0:T(8,128)(2,1)}) %all-gather.4.cloned.1.call-update) | async-done | bytes 8388624 | tf_op jit(solution)/shard_map/all_gather | solution.py:63
  182.8 6.8 %fusion.12 = bf16[48,16,8,128]{3,2,1,0:T(8,128)(2,1)S(1)} fusion(bf16[2048,2048]{1,0:T(8,128)(2,1)} %all-gather.4.cloned.1.call-done, bf16[384,2048]{1,0:T(8,128)(2,1)S(1)} %copy-done, f32[2048]{0:T(1024)S(1)} %convert_element_type.32, f32[384]{0:T(512)S(1)} %add_rsqrt_fusion), kind=kOutput, calls=%fused_computation.22 | convolution fusion | flops 3225157632 | bytes 11544064 | tf_op jit(solution)/shard_map/dot_general | solution.py:69
  190.1 66.2 %while.12 = (s32[]{:T(128)}, bf16[16,384,128]{1,2,0:T(8,128)(2,1)}, bf16[16,384,128]{2,1,0:T(8,128)(2,1)S(1)}, bf16[1536,128]{1,0:T(8,128)(2,1)}, bf16[1536,128]...) while((s32[]{:T(128)}, bf16[16,384,128]{1,2,0:T(8,128)(2,1)}, ...), condition=%wide.region_4.5_spmd.clone, body=%wide.region_1.4_spmd.clone.sunk | while | flops 309165312 | bytes 10055833 | solution.py:52
  190.1 1.9 fusion.47
  194.2 1.9 fusion.47
  198.4 1.9 fusion.47
  201.8 0.7 constant_dynamic-update-slice_fusion.2
  202.5 1.9 fusion.47
  206.0 0.7 constant_dynamic-update-slice_fusion.2
  206.6 1.9 fusion.47
  210.1 0.7 constant_dynamic-update-slice_fusion.2
  210.8 1.9 fusion.47
  214.9 1.9 fusion.47
  219.0 1.9 fusion.47
  222.5 0.7 constant_dynamic-update-slice_fusion.2
  223.2 1.9 fusion.47
  227.3 1.9 fusion.47
  230.8 0.7 constant_dynamic-update-slice_fusion.2
  231.5 1.9 fusion.47
  235.6 1.9 fusion.47
  239.1 0.7 constant_dynamic-update-slice_fusion.2
  239.8 1.9 fusion.47
  244.0 1.9 fusion.47
  248.1 1.9 fusion.47
  252.2 1.9 fusion.47
  255.7 0.7 constant_dynamic-update-slice_fusion.2
  256.3 8.5 %fusion.11 = bf16[384,2048]{1,0:T(8,128)(2,1)} fusion(bf16[384,2048]{1,0:T(8,128)(2,1)S(1)} %copy-done, bf16[384,2048]{0,1:T(8,128)(2,1)} %bitcast.62, bf16[2048,2048]{1,0:T(8,128)(2,1)} %all-gather.6.cloned.1.call-done), kind=kOutput, calls=%fused_computation.19 | convolution fusion | flops 3223584768 | bytes 13107200 | tf_op jit(solution)/shard_map/dot_general | solution.py:101
  (116 shorter events, 32.4 us)
Async XLA Ops:
  7.2 53.2 %copy-start = (bf16[384,2048]{1,0:T(8,128)(2,1)S(1)}, bf16[384,2048]{1,0:T(8,128)(2,1)}, u32[]{:S(2)}) copy-start(bf16[384,2048]{1,0:T(8,128)(2,1)} %param.12) | copy-start | bytes 4718596
  7.2 115.5 %all-gather.8.cloned.1.call-start = ((), (), s32[]{:S(2)}) async-start(), calls=%async_computation.2 | async-start | bytes 6488064 | tf_op jit(solution)/shard_map/all_gather | solution.py:121
  61.1 4.3 %copy-start.3 = (s32[96]{0:T(128)S(1)}, s32[96]{0:T(128)}, u32[]{:S(2)}) copy-start(s32[96]{0:T(128)} %param.19) | copy-start | bytes 1156
  61.1 5.1 %copy-start.2 = (s32[12288]{0:T(1024)S(1)}, s32[12288]{0:T(1024)}, u32[]{:S(2)}) copy-start(s32[12288]{0:T(1024)} %param.18) | copy-start | bytes 147460
  62.6 120.3 %all-gather.4.cloned.1.call-start = ((), (), s32[]{:S(2)}) async-start(), calls=%async_computation | async-start | bytes 8650752 | tf_op jit(solution)/shard_map/all_gather | solution.py:63
  63.3 193.0 %all-gather.6.cloned.1.call-start = ((), (), s32[]{:S(2)}) async-start(), calls=%async_computation.1 | async-start | bytes 8650752 | tf_op jit(solution)/shard_map/all_gather | solution.py:103
  63.4 5.0 %collective-permute-start = (bf16[384,256]{0,1:T(8,128)(2,1)}, bf16[384,256]{0,1:T(8,128)(2,1)S(1)}, u32[]{:S(2)}, u32[]{:S(2)}) collective-permute-start(bf16[384,256]{0,1:T(8,128)(2,1)} %pad_maximum_fusion), channel_id=1, source_target_pairs={{0,8},{8,16},{16,24},{24,32},{32,40},{40,48},{48,56},{56,64},{64,7... | collective-permute-start | bytes 589832 | tf_op jit(solution)/shard_map/ppermute | solution.py:15
  68.4 6.7 %collective-permute-start.1 = (bf16[384,256]{0,1:T(8,128)(2,1)S(1)}, bf16[384,256]{0,1:T(8,128)(2,1)S(1)}, u32[]{:S(2)}, u32[]{:S(2)}) collective-permute-start(bf16[384,256]{0,1:T(8,128)(2,1)S(1)} %collective-permute-done), channel_id=1, source_target_pairs={{0,8},{8,16},{16,24},{24,32},{32,40},{40,48},{48,56},{56,64},{64,7... | collective-permute-start | bytes 589832 | tf_op jit(solution)/shard_map/ppermute | solution.py:15
  75.1 7.9 %collective-permute-start.2 = (bf16[384,256]{0,1:T(8,128)(2,1)S(1)}, bf16[384,256]{0,1:T(8,128)(2,1)S(1)}, u32[]{:S(2)}, u32[]{:S(2)}) collective-permute-start(bf16[384,256]{0,1:T(8,128)(2,1)S(1)} %collective-permute-done.1), channel_id=1, source_target_pairs={{0,8},{8,16},{16,24},{24,32},{32,40},{40,48},{48,56},{56,64},{64,7... | collective-permute-start | bytes 589832 | tf_op jit(solution)/shard_map/ppermute | solution.py:15
  192.0 1.0 copy-start.1
  196.1 1.0 copy-start.1
  200.2 1.0 copy-start.1
  204.4 1.0 copy-start.1
  208.5 1.0 copy-start.1
  212.6 1.0 copy-start.1
  216.7 1.0 copy-start.1
  220.9 1.0 copy-start.1
  225.1 1.0 copy-start.1
  229.2 1.0 copy-start.1
  233.4 1.0 copy-start.1
  237.5 1.0 copy-start.1
  241.7 1.0 copy-start.1
  245.8 1.0 copy-start.1
  249.9 1.0 copy-start.1
  254.1 1.0 copy-start.1
Sparse Core Ops, SparseCore 0:
  62.7 59.9 all-gather.7
  125.2 57.5 all-gather.3
  185.4 57.5 all-gather.5
where the time goes:
time: 273 us; the launch traced here: 271 us
  waiting for transfers between devices  89.7 us (33%)
  matrix products  54.3 us (20%)
  blocking collectives  50.5 us (18%)
  local copies, waits for them, and re-layouts  37.7 us (14%)
  other arithmetic  14.3 us (5%)
  between operations  13.9 us (5%)
  starting transfers between devices  10.7 us (4%)
    all_gather x1, waiting for transfers between devices, shards(): lax.all_gather(w_query, 'seq', axis=0, tiled=True)  45.4 us
    all_gather x1, waiting for transfers between devices, shards(): piece = lax.all_gather(stacked, 'seq', axis=0, tiled=True)  37.7 us
    dot_general x16, matrix products, one_head(): lax.dot_general(query_head, key_rows, (((1,), (1,)), ((), ())), preferred...  30 us
    all_gather x1, blocking collectives, shards(): lax.all_gather(w_value, 'seq', axis=0, tiled=True)  26.4 us
    all_gather x1, blocking collectives, shards(): lax.all_gather(w_key, 'seq', axis=0, tiled=True)  24.1 us
    dynamic_update_slice x32, local copies, waits for them, and re-layouts, attend_block(): result = lax.map(one_head, per_head)  12.5 us
    ppermute x3, starting transfers between devices, shifted(): return lax.ppermute(array, axis, pairs)  10.5 us
    all_gather x1, local copies, waits for them, and re-layouts, shards(): piece = lax.all_gather(stacked, 'seq', axis=0, tiled=True)  8.63 us
  transfers between devices with their start and end apart: 6, of which 4 were waited for; matrix products, arithmetic and copies ran while one was open for 31% of the time, Pallas kernels for 0%

commit v1 on v0

--- a/solution.py
+++ b/solution.py
@@ -7,6 +7,14 @@
 CACHE_BLK = 128
 REACH = 3
 EPSILON = 1e-06
+
+
+def gather_by_exchange(array, axis, dim):
+    size = lax.axis_size(axis)
+    repeats = [size if d == dim else 1 for d in range(array.ndim)]
+    return lax.all_to_all(
+        jnp.tile(array, repeats), axis, split_axis=dim, concat_axis=dim, tiled=True
+    )
 
 
 def shifted(array, axis, by):
@@ -62,7 +70,7 @@
     pieces = (
         lax.all_gather(w_query, "seq", axis=0, tiled=True),
         lax.all_gather(w_key, "seq", axis=0, tiled=True),
-        lax.all_gather(w_value, "seq", axis=0, tiled=True),
+        gather_by_exchange(w_value, "seq", 0),
     )
     columns = normed
     query_sum, key_sum, value_sum = tuple(

time: 273 us -> 258 us (0.945)
  blocking collectives: 50.5 us -> 27.6 us
  starting transfers between devices: 10.7 us -> 19.5 us
    all_gather x1 -> x0, blocking collectives: 26.4 us -> none  [shards(): lax.all_gather(w_value, 'seq', axis=0, tiled=True)]
    all_to_all x0 -> x1, starting transfers between devices: none -> 8.59 us  [gather_by_exchange(): lax.all_to_all(jnp.tile(array, repeats), axis, split_axis=dim, concat_axi...]
    all_gather x1, waiting for transfers between devices: 37.7 us -> 33.3 us  [shards(): piece = lax.all_gather(stacked, 'seq', axis=0, tiled=True)]
    ppermute x3, waiting for transfers between devices: 5.86 us -> 9.39 us  [shifted(): return lax.ppermute(array, axis, pairs)]
    all_gather x1, blocking collectives: 24.1 us -> 27.6 us  [shards(): lax.all_gather(w_key, 'seq', axis=0, tiled=True)]
  transfers between devices with their start and end apart: 6 -> 7, of which waited for: 4 -> 5; matrix products, arithmetic and copies ran while one was open for 31% -> 33% of each run, Pallas kernels for 0% -> 0%
where the time goes in v1:
time: 258 us; the launch traced here: 256 us
  waiting for transfers between devices  89.5 us (35%)
  matrix products  54.3 us (21%)
  local copies, waits for them, and re-layouts  39.3 us (15%)
  blocking collectives  27.6 us (11%)
  starting transfers between devices  19.5 us (8%)
  between operations  14 us (5%)
  other arithmetic  11.9 us (5%)
    all_gather x1, waiting for transfers between devices, shards(): lax.all_gather(w_query, 'seq', axis=0, tiled=True)  45.4 us
    all_gather x1, waiting for transfers between devices, shards(): piece = lax.all_gather(stacked, 'seq', axis=0, tiled=True)  33.3 us
    dot_general x16, matrix products, one_head(): lax.dot_general(query_head, key_rows, (((1,), (1,)), ((), ())), preferred...  30 us
    all_gather x1, blocking collectives, shards(): lax.all_gather(w_key, 'seq', axis=0, tiled=True)  27.6 us
    dynamic_update_slice x32, local copies, waits for them, and re-layouts, attend_block(): result = lax.map(one_head, per_head)  12.5 us
    ppermute x3, starting transfers between devices, shifted(): return lax.ppermute(array, axis, pairs)  10.7 us
    ppermute x3, waiting for transfers between devices, shifted(): return lax.ppermute(array, axis, pairs)  9.39 us
    all_gather x1, local copies, waits for them, and re-layouts, shards(): piece = lax.all_gather(stacked, 'seq', axis=0, tiled=True)  8.62 us
  transfers between devices with their start and end apart: 7, of which 5 were waited for; matrix products, arithmetic and copies ran while one was open for 33% of the time, Pallas kernels for 0%

profile of v1, /device:TPU:1, one launch (start us, length us, event | category | flops | bytes accessed | tf_op | source)
XLA Modules:
  0.0 256.3 jit_solution(11627310281379975193)
XLA Ops:
  7.2 1.7 tile.2
  8.9 8.6 %all-to-all-start = ((bf16[32,64,128]{2,1,0:T(8,128)(2,1)}), bf16[32,64,128]{2,1,0:T(8,128)(2,1)S(1)}, u32[]{:S(2)}, u32[]{:S(2)}) async-start(bf16[32,64,128]{2,1,0:T(8,128)(2,1)} %tile.2), calls=%async_computation | async-start | bytes 1048576 | tf_op jit(solution)/shard_map/all_to_all | solution.py:15
  18.0 27.6 %all_gather.13 = bf16[2048,128]{1,0:T(8,128)(2,1)S(1)} all-gather(bf16[64,128]{1,0:T(8,128)(2,1)S(1)} %copy-done.3), channel_id=1, replica_groups=mesh['seq'=32,'grp'=8] {'seq'}, dimensions={0}, use_global_device_ids=true | all-gather | bytes 540672 | tf_op jit(solution)/shard_map/all_gather | solution.py:72
  45.6 0.7 convolution_convert_fusion.2
  46.4 0.7 convolution_convert_fusion.1
  47.1 0.7 pad_maximum_fusion
  47.9 0.7 all-gather.4.cloned.1.call-update
  48.6 0.7 all-gather.6.cloned.1.call-update
  50.2 1.9 fusion.23
  52.1 1.9 collective-permute-start
  54.1 2.8 %collective-permute-done = bf16[384,256]{0,1:T(8,128)(2,1)S(1)} collective-permute-done((bf16[384,256]{0,1:T(8,128)(2,1)}, bf16[384,256]{0,1:T(8,128)(2,1)S(1)}, u32[]{:S(2)}, u32[]{:S(2)}) %collective-permute-start) | collective-permute-done | bytes 196640 | tf_op jit(solution)/shard_map/ppermute | solution.py:23
  56.9 4.3 %collective-permute-start.1 = (bf16[384,256]{0,1:T(8,128)(2,1)S(1)}, bf16[384,256]{0,1:T(8,128)(2,1)S(1)}, u32[]{:S(2)}, u32[]{:S(2)}) collective-permute-start(bf16[384,256]{0,1:T(8,128)(2,1)S(1)} %collective-permute-done), channel_id=1, source_target_pairs={{0,8},{8,16},{16,24},{24,32},{32,40},{40,48},{48,56},{56,64},{64,7... | collective-permute-start | bytes 589832 | tf_op jit(solution)/shard_map/ppermute | solution.py:23
  61.2 3.1 %collective-permute-done.1 = bf16[384,256]{0,1:T(8,128)(2,1)S(1)} collective-permute-done((bf16[384,256]{0,1:T(8,128)(2,1)S(1)}, bf16[384,256]{0,1:T(8,128)(2,1)S(1)}, u32[]{:S(2)}, u32[]{:S(2)}) %collective-permute-start.1) | collective-permute-done | bytes 196640 | tf_op jit(solution)/shard_map/ppermute | solution.py:23
  64.3 4.6 %collective-permute-start.2 = (bf16[384,256]{0,1:T(8,128)(2,1)S(1)}, bf16[384,256]{0,1:T(8,128)(2,1)S(1)}, u32[]{:S(2)}, u32[]{:S(2)}) collective-permute-start(bf16[384,256]{0,1:T(8,128)(2,1)S(1)} %collective-permute-done.1), channel_id=1, source_target_pairs={{0,8},{8,16},{16,24},{24,32},{32,40},{40,48},{48,56},{56,64},{64,7... | collective-permute-start | bytes 589832 | tf_op jit(solution)/shard_map/ppermute | solution.py:23
  68.9 3.5 %collective-permute-done.2 = bf16[384,256]{0,1:T(8,128)(2,1)S(1)} collective-permute-done((bf16[384,256]{0,1:T(8,128)(2,1)S(1)}, bf16[384,256]{0,1:T(8,128)(2,1)S(1)}, u32[]{:S(2)}, u32[]{:S(2)}) %collective-permute-start.2) | collective-permute-done | bytes 196640 | tf_op jit(solution)/shard_map/ppermute | solution.py:23
  72.5 0.9 copy.20
  73.4 0.9 copy.21
  74.4 33.3 %all-gather.8.cloned.1.call-done = bf16[12288,256]{0,1:T(8,128)(2,1)} async-done(((bf16[384,256]{0,1:T(8,128)(2,1)}), bf16[12288,256]{0,1:T(8,128)(2,1)}) %all-gather.8.cloned.1.call-update) | async-done | bytes 6291472 | tf_op jit(solution)/shard_map/all_gather | solution.py:129
  107.7 8.6 %copy.23 = bf16[12288,256]{1,0:T(8,128)(2,1)} copy(bf16[12288,256]{0,1:T(8,128)(2,1)} %all-gather.8.cloned.1.call-done) | data formatting | bytes 12582912 | tf_op jit(solution)/shard_map/all_gather | solution.py:129
  116.3 5.3 %gather_fusion = bf16[384,256]{1,0:T(8,128)(2,1)S(1)} fusion(bf16[12288,256]{1,0:T(8,128)(2,1)} %copy.23, s32[1024]{0:T(1024)S(1)} %pad_clamp_fusion), kind=kCustom, calls=%fused_computation | custom fusion | bytes 394752 | tf_op jit(solution)/shard_map/jit(_take)/gather | solution.py:131
  121.5 0.8 select_select_fusion
  122.4 45.4 %all-gather.4.cloned.1.call-done = bf16[2048,2048]{1,0:T(8,128)(2,1)} async-done(((bf16[64,2048]{1,0:T(8,128)(2,1)}), bf16[2048,2048]{1,0:T(8,128)(2,1)}) %all-gather.4.cloned.1.call-update) | async-done | bytes 8388624 | tf_op jit(solution)/shard_map/all_gather | solution.py:71
  167.8 6.8 %fusion.12 = bf16[48,16,8,128]{3,2,1,0:T(8,128)(2,1)S(1)} fusion(bf16[2048,2048]{1,0:T(8,128)(2,1)} %all-gather.4.cloned.1.call-done, bf16[384,2048]{1,0:T(8,128)(2,1)S(1)} %copy-done, f32[2048]{0:T(1024)S(1)} %convert_element_type.32, f32[384]{0:T(512)S(1)} %add_rsqrt_fusion), kind=kOutput, calls=%fused_computation.22 | convolution fusion | flops 3225157632 | bytes 11544064 | tf_op jit(solution)/shard_map/dot_general | solution.py:77
  175.1 66.2 %while.12 = (s32[]{:T(128)}, bf16[16,384,128]{1,2,0:T(8,128)(2,1)}, bf16[16,384,128]{2,1,0:T(8,128)(2,1)S(1)}, bf16[1536,128]{1,0:T(8,128)(2,1)}, bf16[1536,128]...) while((s32[]{:T(128)}, bf16[16,384,128]{1,2,0:T(8,128)(2,1)}, ...), condition=%wide.region_4.5_spmd.clone, body=%wide.region_1.4_spmd.clone.sunk | while | flops 309165312 | bytes 10055833 | solution.py:60
  175.1 1.9 fusion.47
  178.6 0.7 constant_dynamic-update-slice_fusion.2
  179.2 1.9 fusion.47
  182.7 0.7 constant_dynamic-update-slice_fusion.2
  183.4 1.9 fusion.47
  186.9 0.7 constant_dynamic-update-slice_fusion.2
  187.5 1.9 fusion.47
  191.6 1.9 fusion.47
  195.8 1.9 fusion.47
  199.2 0.7 constant_dynamic-update-slice_fusion.2
  199.9 1.9 fusion.47
  203.4 0.7 constant_dynamic-update-slice_fusion.2
  204.0 1.9 fusion.47
  208.2 1.9 fusion.47
  212.3 1.9 fusion.47
  215.8 0.7 constant_dynamic-update-slice_fusion.2
  216.4 1.9 fusion.47
  220.6 1.9 fusion.47
  224.8 1.9 fusion.47
  229.0 1.9 fusion.47
  233.1 1.9 fusion.47
  236.5 0.7 constant_dynamic-update-slice_fusion.2
  237.2 1.9 fusion.47
  241.3 8.5 %fusion.11 = bf16[384,2048]{1,0:T(8,128)(2,1)} fusion(bf16[384,2048]{1,0:T(8,128)(2,1)S(1)} %copy-done, bf16[384,2048]{0,1:T(8,128)(2,1)} %bitcast.64, bf16[2048,2048]{1,0:T(8,128)(2,1)} %all-gather.6.cloned.1.call-done), kind=kOutput, calls=%fused_computation.19 | convolution fusion | flops 3223584768 | bytes 13107200 | tf_op jit(solution)/shard_map/dot_general | solution.py:109
  (122 shorter events, 33.4 us)
Async XLA Ops:
  7.2 10.4 %copy-start = (bf16[384,2048]{1,0:T(8,128)(2,1)S(1)}, bf16[384,2048]{1,0:T(8,128)(2,1)}, u32[]{:S(2)}) copy-start(bf16[384,2048]{1,0:T(8,128)(2,1)} %param.12) | copy-start | bytes 4718596
  7.2 10.8 %copy-start.3 = (bf16[64,128]{1,0:T(8,128)(2,1)S(1)}, bf16[64,128]{1,0:T(8,128)(2,1)}, u32[]{:S(2)}) copy-start(bf16[64,128]{1,0:T(8,128)(2,1)} %param.15) | copy-start | bytes 49156
  7.2 38.4 %copy-start.4 = (bf16[2048]{0:T(1024)(128)(2,1)S(1)}, bf16[2048]{0:T(1024)(128)(2,1)}, u32[]{:S(2)}) copy-start(bf16[2048]{0:T(1024)(128)(2,1)} %param.13) | copy-start | bytes 12292
  8.9 37.4 %all-to-all-start = ((bf16[32,64,128]{2,1,0:T(8,128)(2,1)}), bf16[32,64,128]{2,1,0:T(8,128)(2,1)S(1)}, u32[]{:S(2)}, u32[]{:S(2)}) async-start(bf16[32,64,128]{2,1,0:T(8,128)(2,1)} %tile.2), calls=%async_computation | async-start | bytes 1048576 | tf_op jit(solution)/shard_map/all_to_all | solution.py:15
  17.5 90.1 %all-gather.8.cloned.1.call-start = ((), (), s32[]{:S(2)}) async-start(), calls=%async_computation.3 | async-start | bytes 6488064 | tf_op jit(solution)/shard_map/all_gather | solution.py:129
  46.4 3.0 %copy-start.5 = (s32[96]{0:T(128)S(1)}, s32[96]{0:T(128)}, u32[]{:S(2)}) copy-start(s32[96]{0:T(128)} %param.19) | copy-start | bytes 1156
  46.4 3.8 %copy-start.2 = (s32[12288]{0:T(1024)S(1)}, s32[12288]{0:T(1024)}, u32[]{:S(2)}) copy-start(s32[12288]{0:T(1024)} %param.18) | copy-start | bytes 147460
  47.8 120.0 %all-gather.4.cloned.1.call-start = ((), (), s32[]{:S(2)}) async-start(), calls=%async_computation.1 | async-start | bytes 8650752 | tf_op jit(solution)/shard_map/all_gather | solution.py:71
  48.6 192.7 %all-gather.6.cloned.1.call-start = ((), (), s32[]{:S(2)}) async-start(), calls=%async_computation.2 | async-start | bytes 8650752 | tf_op jit(solution)/shard_map/all_gather | solution.py:111
  52.1 4.8 %collective-permute-start = (bf16[384,256]{0,1:T(8,128)(2,1)}, bf16[384,256]{0,1:T(8,128)(2,1)S(1)}, u32[]{:S(2)}, u32[]{:S(2)}) collective-permute-start(bf16[384,256]{0,1:T(8,128)(2,1)} %pad_maximum_fusion), channel_id=1, source_target_pairs={{0,8},{8,16},{16,24},{24,32},{32,40},{40,48},{48,56},{56,64},{64,7... | collective-permute-start | bytes 589832 | tf_op jit(solution)/shard_map/ppermute | solution.py:23
  56.9 7.4 %collective-permute-start.1 = (bf16[384,256]{0,1:T(8,128)(2,1)S(1)}, bf16[384,256]{0,1:T(8,128)(2,1)S(1)}, u32[]{:S(2)}, u32[]{:S(2)}) collective-permute-start(bf16[384,256]{0,1:T(8,128)(2,1)S(1)} %collective-permute-done), channel_id=1, source_target_pairs={{0,8},{8,16},{16,24},{24,32},{32,40},{40,48},{48,56},{56,64},{64,7... | collective-permute-start | bytes 589832 | tf_op jit(solution)/shard_map/ppermute | solution.py:23
  64.3 8.1 %collective-permute-start.2 = (bf16[384,256]{0,1:T(8,128)(2,1)S(1)}, bf16[384,256]{0,1:T(8,128)(2,1)S(1)}, u32[]{:S(2)}, u32[]{:S(2)}) collective-permute-start(bf16[384,256]{0,1:T(8,128)(2,1)S(1)} %collective-permute-done.1), channel_id=1, source_target_pairs={{0,8},{8,16},{16,24},{24,32},{32,40},{40,48},{48,56},{56,64},{64,7... | collective-permute-start | bytes 589832 | tf_op jit(solution)/shard_map/ppermute | solution.py:23
  177.0 1.0 copy-start.1
  181.1 1.0 copy-start.1
  185.3 1.0 copy-start.1
  189.4 1.0 copy-start.1
  193.5 1.0 copy-start.1
  197.6 1.0 copy-start.1
  201.7 1.0 copy-start.1
  205.9 1.0 copy-start.1
  210.0 1.0 copy-start.1
  214.2 1.0 copy-start.1
  218.3 1.0 copy-start.1
  222.5 1.0 copy-start.1
  226.7 1.0 copy-start.1
  230.8 1.0 copy-start.1
  234.9 1.0 copy-start.1
  239.1 1.0 copy-start.1
Sparse Core Ops, SparseCore 0:
  48.0 59.6 all-gather.7
  110.2 57.5 all-gather.3
  170.4 57.5 all-gather.5
